TPU v7x, 32 devices: a whole 2x2x4 slice. The times are simulated.
32 devices in a mesh: slab: 8 (over z, x), depth: 4 (over y, core).
Axes of the slice: x: 2, y: 2, z: 4, core: 2. Of those that a mesh axis runs over, the one named last changes fastest.
Arguments:
- right_side: float32 [3, 8, 8, 32, 256], P(None, None, 'slab', 'depth'), may hold values from -4 to 9
- smoother: float32 [3, 8, 32, 256], P(None, 'slab', 'depth'), may hold values from 0.1 to 1
- material: int32 [8, 32, 256], P('slab', 'depth'), may hold values from 0 to 15
- moduli: float32 [16], replicated, may hold values from 0.25 to 4
- element_matrix: float32 [24, 24], replicated, may hold values from -0.15 to 3, as said below
- coarse_inverse: float32 [24, 24], replicated, may hold values from -0.2 to 1.2, as said below
- surface_map: int32 [8, 256], P('slab'), may hold values from 0 to 2047, as said below
- line_of_sight: float32 [3, 8, 256], P(None, 'slab'), may hold values from -3 to 3
Outputs:
- residual: float32 [3, 8, 8, 32, 256], P(None, None, 'slab', 'depth')
- pixels: float32 [8, 2048], P('depth', 'slab')
Inputs may be any that keep to these rules, and one draw needn't show every extreme that they name: `element_matrix`: symmetric. `coarse_inverse`: symmetric. `surface_map`: pixel p lies in tile p // 256. At most 64 surface nodes of one slab block lie in one tile, and some tile holds exactly 64 surface nodes of every slab block.
All inputs are finite; a program needn't handle non-finite values.
Results may differ from a plain program's by a relative error of at most 0.0003.
Values sent between devices are 32-bit elements; how exact they have to be, the bound alone decides.
No kernel may reach another device: no remote copies, remote signals or barrier semaphores. Data moves between devices by JAX's collectives and lax.ppermute only.
A program may use at most 64 MiB of HBM per device.

v0:
```python
import jax
import jax.numpy as jnp
from jax import lax
from jax.sharding import PartitionSpec as P

PIX = 256


def extended(array, sides, width):
    for axis, dim in sides:
        peers, length = (lax.axis_size(axis), array.shape[dim])
        up = [(i, (i + 1) % peers) for i in range(peers - 1)]
        down = [(j, i) for i, j in up]
        last = lax.slice_in_dim(array, length - width, length, axis=dim)
        initial = lax.slice_in_dim(array, 0, width, axis=dim)
        before = lax.ppermute(last, axis, up)
        after = lax.ppermute(initial, axis, down)
        array = jnp.concatenate([before, array, after], axis=dim)
    return array


def broadcast(value, axis, source):
    kept = jnp.where(lax.axis_index(axis) == source, value, 0).astype(value.dtype)
    return lax.psum(kept, axis)


def stiffness(padded_field, padded_moduli, element_matrix):
    sources = padded_field.shape[1]
    span_x = padded_field.shape[2] - 1
    span_z = padded_field.shape[3] - 1
    span_y = padded_moduli.shape[2]
    corners = []
    for corner in range(8):
        along_x, along_z, along_y = (corner // 4, corner // 2 % 2, corner % 2)
        corners.append(
            padded_field[
                :,
                :,
                along_x : along_x + span_x,
                along_z : along_z + span_z,
                along_y : along_y + span_y,
            ]
        )
    stacked = jnp.stack(corners, 0).reshape(24, -1)
    forces = jnp.dot(
        element_matrix, stacked, precision=lax.Precision.HIGHEST, preferred_element_type=jnp.float32
    )
    forces = forces.reshape(8, 3, sources, span_x, span_z, span_y) * padded_moduli[1:, 1:, :]
    forces = jnp.pad(forces, ((0, 0), (0, 0), (0, 0), (0, 0), (0, 0), (0, 1)))
    summed = jnp.zeros((3, sources, span_x - 1, span_z - 1, span_y), jnp.float32)
    for corner in range(8):
        along_x, along_z, along_y = (corner // 4, corner // 2 % 2, corner % 2)
        summed = (
            summed
            + forces[
                corner,
                :,
                :,
                1 - along_x : 1 - along_x + span_x - 1,
                1 - along_z : 1 - along_z + span_z - 1,
                1 - along_y : 1 - along_y + span_y,
            ]
        )
    return summed


def pack_slots(values, targets, n_slab):
    node_count = values.shape[1]
    capacity = 2 * node_count // n_slab
    tile_owner = targets // PIX
    in_tile = targets % PIX
    onehot = (tile_owner[:, None] == jnp.arange(n_slab, dtype=jnp.int32)[None]).astype(jnp.int32)
    slot_rank = jnp.sum((jnp.cumsum(onehot, axis=0) - 1) * onehot, axis=1)
    send_vals = (
        jnp.zeros((values.shape[0], capacity, n_slab), jnp.float32)
        .at[:, slot_rank, tile_owner]
        .set(values)
    )
    send_ids = (
        jnp.zeros((1, capacity, n_slab), jnp.float32)
        .at[0, slot_rank, tile_owner]
        .set(in_tile.astype(jnp.float32))
    )
    return (send_vals, send_ids)


def bin_pixels(got_vals, got_ids):
    pixel_index = got_ids.reshape(-1).astype(jnp.int32)
    rows = got_vals.shape[0]
    return jnp.zeros((rows, PIX), jnp.float32).at[:, pixel_index].add(got_vals.reshape(rows, -1))


def body(
    right_side,
    smoother,
    material,
    moduli,
    element_matrix,
    coarse_inverse,
    surface_map,
    line_of_sight,
):
    components, sources, width_x, width_z, width_y = right_side.shape
    n_slab = lax.axis_size("slab")
    n_depth = lax.axis_size("depth")
    slab_rank = lax.axis_index("slab")
    depth_rank = lax.axis_index("depth")
    levels = jnp.arange(moduli.shape[0], dtype=jnp.int32)
    modulus_field = jnp.sum(
        jnp.where(material[None] == levels[:, None, None, None], moduli[:, None, None, None], 0.0),
        axis=0,
    )
    weights = smoother[:, None]
    stacked = jnp.concatenate(
        [
            right_side.reshape(components * sources, width_x, width_z, width_y),
            smoother,
            modulus_field[None],
        ],
        0,
    )
    source_pad = extended(stacked, (("slab", 1), ("depth", 2)), 1)
    agg_nodes = float(width_x * width_z * n_depth * width_y)
    block_sums = jnp.sum(right_side, axis=(2, 3, 4))
    placed = jnp.where(
        jnp.arange(n_slab, dtype=jnp.int32)[:, None, None] == slab_rank, block_sums[None], 0.0
    )
    placed = placed.reshape(components * n_slab, sources)
    coarse_sum = lax.psum(placed, ("slab", "depth"))
    coarse_vec = coarse_sum / agg_nodes
    correction = jnp.dot(
        coarse_inverse,
        coarse_vec,
        precision=lax.Precision.HIGHEST,
        preferred_element_type=jnp.float32,
    )
    by_block = correction.reshape(n_slab, components, sources)
    own_corr = lax.dynamic_index_in_dim(by_block, slab_rank, 0, keepdims=False)
    direction = weights * right_side + own_corr[:, :, None, None, None]
    numerator = lax.psum(jnp.sum(right_side * direction, axis=(0, 2, 3, 4)), ("slab", "depth"))
    field_pad = source_pad[: components * sources].reshape(
        components, sources, width_x + 2, width_z + 2, width_y
    )
    weight_pad = source_pad[components * sources : components * sources + components]
    moduli_pad = source_pad[components * sources + components]
    low_block = jnp.maximum(slab_rank - 1, 0)
    high_block = jnp.minimum(slab_rank + 1, n_slab - 1)
    low_corr = jnp.where(
        slab_rank > 0, lax.dynamic_index_in_dim(by_block, low_block, 0, keepdims=False), 0.0
    )
    high_corr = jnp.where(
        slab_rank < n_slab - 1,
        lax.dynamic_index_in_dim(by_block, high_block, 0, keepdims=False),
        0.0,
    )
    row_corr = jnp.concatenate([low_corr[None], own_corr[None], high_corr[None]], 0)
    row_corr = jnp.transpose(row_corr, (1, 2, 0))
    depth_mask = jnp.ones((width_z + 2,), jnp.float32)
    depth_mask = depth_mask.at[0].set(jnp.where(depth_rank > 0, 1.0, 0.0))
    depth_mask = depth_mask.at[width_z + 1].set(jnp.where(depth_rank < n_depth - 1, 1.0, 0.0))
    padded = (
        weight_pad[:, None] * field_pad
        + row_corr[:, :, :, None, None] * depth_mask[None, None, None, :, None]
    )
    padded = jnp.pad(padded, ((0, 0), (0, 0), (0, 0), (0, 0), (1, 0)))
    applied = stiffness(padded, moduli_pad, element_matrix)
    denominator = lax.psum(jnp.sum(direction * applied, axis=(0, 2, 3, 4)), ("slab", "depth"))
    step_size = numerator / denominator
    residual = right_side - step_size[None, :, None, None, None] * applied
    surface = step_size[None, :, None, None] * direction[:, :, :, width_z - 1, :]
    projected = jnp.sum(line_of_sight[:, None] * surface, axis=0).reshape(sources, -1)
    projected = broadcast(projected, "depth", n_depth - 1)
    targets = surface_map.reshape(-1)
    per_row = sources // n_depth
    send_vals, send_ids = pack_slots(projected, targets, n_slab)
    got_vals, got_ids = (
        lax.all_to_all(send_vals, "slab", split_axis=2, concat_axis=2, tiled=True),
        lax.all_to_all(send_ids, "slab", split_axis=2, concat_axis=2, tiled=True),
    )
    binned = bin_pixels(got_vals, got_ids)
    pixels = lax.dynamic_slice_in_dim(binned, depth_rank * per_row, per_row, 0)
    return (residual, pixels)


def solution(mesh):
    return jax.shard_map(
        body,
        mesh=mesh,
        in_specs=(
            P(None, None, "slab", "depth", None),
            P(None, "slab", "depth", None),
            P("slab", "depth", None),
            P(),
            P(),
            P(),
            P("slab", None),
            P(None, "slab", None),
        ),
        out_specs=(P(None, None, "slab", "depth", None), P("depth", "slab")),
        check_vma=False,
    )
```

profile of v0, /device:TPU:0, one launch (start us, length us, event | category | flops | bytes accessed | tf_op | source)
XLA Modules:
  0.0 215.8 jit_solution(9086493570849835887)
XLA Ops:
  0.7 0.8 select_reduce_fusion
  1.5 1.0 pad_maximum_fusion.1
  2.5 1.3 collective-permute-start.1
  3.8 5.5 %collective-permute-start = (f32[28,1,8,256]{3,2,1,0:T(8,128)S(1)}, f32[28,1,8,256]{3,2,1,0:T(8,128)S(1)}, u32[]{:S(2)}, u32[]{:S(2)}) collective-permute-start(f32[28,1,8,256]{3,2,1,0:T(8,128)S(1)} %pad_maximum_fusion.1), channel_id=1, source_target_pairs={{0,4},{4,8},{8,12},{12,16},{16,20},{20,24},{24,28},{1,5},{5,9},{9,... | collective-permute-start | bytes 688136 | tf_op jit(solution)/shard_map/ppermute | solution.py:16
  9.3 0.7 and_select_fusion.2
  10.0 0.7 fusion.34
  10.7 0.6 reduce-window.6
  11.6 0.7 or_select_fusion
  12.3 0.6 broadcast.316
  12.9 38.7 %scatter_fusion = f32[64,8]{0,1:T(8,128)} fusion(f32[64,8]{0,1:T(8,128)} %broadcast.316, s32[256]{0:T(256)S(1)} %bitcast.120, f32[256]{0:T(256)S(1)} %get-tuple-element.49), kind=kCustom, calls=%fused_computation | custom fusion | bytes 5120 | tf_op jit(solution)/shard_map/scatter | solution.py:82
  51.6 6.2 %all-to-all-start = ((f32[1,64,8]{1,0,2:T(1,128)}), f32[1,64,8]{1,0,2:T(1,128)S(1)}, u32[]{:S(2)}, u32[]{:S(2)}) async-start(f32[1,64,8]{1,0,2:T(1,128)} %bitcast.34), calls=%async_computation | async-start | bytes 8192 | tf_op jit(solution)/shard_map/all_to_all | solution.py:178
  57.8 1.1 reduce_sum.56
  59.2 40.8 %psum.28 = f32[24,8]{1,0:T(8,128)S(1)} all-reduce(f32[24,8]{1,0:T(8,128)S(1)} %broadcast_select_fusion), channel_id=1, replica_groups=mesh['slab'=8,'depth'=4] {'slab','depth'}, use_global_device_ids=true, to_apply=%region_1.2 | all-reduce | flops 192 | bytes 1536 | tf_op jit(solution)/shard_map/psum | solution.py:129
  100.0 0.9 convolution_bitcast_fusion.1
  101.2 0.4 copy-done.6
  101.7 1.3 copy.99
  103.2 0.9 pad_maximum_fusion.7
  104.1 1.3 collective-permute-start.2
  105.4 1.3 collective-permute-start.3
  106.7 0.5 compare_select_fusion
  107.3 3.9 %collective-permute-done.3 = f32[28,3,1,256]{3,2,1,0:T(1,128)S(1)} collective-permute-done((f32[28,3,1,256]{3,2,1,0:T(1,128)S(1)}, f32[28,3,1,256]{3,2,1,0:T(1,128)S(1)}, u32[]{:S(2)}, u32[]{:S(2)}) %collective-permute-start.3) | collective-permute-done | bytes 86048 | tf_op jit(solution)/shard_map/ppermute | solution.py:17
  111.2 0.6 slice.139
  111.8 0.3 pad_maximum_fusion
  112.2 0.2 multiply_add_fusion
  112.4 1.1 fusion.1
  113.6 1.0 fusion.11
  114.6 1.2 fusion.3
  115.7 1.0 fusion.10
  116.7 1.1 fusion.5
  117.9 0.9 fusion.9
  118.8 1.2 fusion.7
  120.0 1.0 fusion.8
  121.0 3.8 %reshape.438 = f32[24,36864]{1,0:T(8,128)S(1)} reshape(f32[8,3,8,2,9,256]{5,4,3,2,1,0:T(8,128)} %fusion.8) | data formatting | bytes 7077888 | tf_op jit(solution)/shard_map/reshape | solution.py:44
  124.8 4.9 %convolution_bitcast_fusion = f32[24,36864]{1,0:T(8,128)} fusion(f32[24,36864]{1,0:T(8,128)S(1)} %reshape.438, f32[24,24]{1,0:T(8,128)S(1)} %copy-done), kind=kOutput, calls=%fused_computation.3 | convolution fusion | flops 254803968 | bytes 7080192 | tf_op jit(solution)/shard_map/dot_general | solution.py:45
  129.8 5.2 %reshape.439 = f32[8,3,8,2,9,256]{5,4,3,2,1,0:T(8,128)} reshape(f32[24,36864]{1,0:T(8,128)} %convolution_bitcast_fusion) | data formatting | bytes 7077888 | tf_op jit(solution)/shard_map/reshape | solution.py:48
  135.0 3.6 %broadcast_multiply_fusion = f32[8,3,8,2,9,256]{5,4,3,2,1,0:T(8,128)S(1)} fusion(f32[8,3,8,2,9,256]{5,4,3,2,1,0:T(8,128)} %reshape.439, f32[2,9,256]{2,1,0:T(8,128)S(1)} %copy-done.5), kind=kLoop, calls=%fused_computation.8 | loop fusion | flops 884736 | bytes 7096320 | tf_op jit(solution)/shard_map/mul | solution.py:48
  138.7 0.4 fusion.19
  139.1 40.8 %all-reduce.3 = (f32[8]{0:T(128)S(1)}, f32[8]{0:T(128)S(1)}) all-reduce(f32[8]{0:T(128)S(1)} %get-tuple-element.39, f32[8]{0:T(128)S(1)} %get-tuple-element.38), channel_id=1, replica_groups=mesh['slab'=8,'depth'=4] {'slab','depth'}, use_global_device_ids=true, to_apply=%region_3.4 | all-reduce | flops 16 | bytes 128 | tf_op jit(solution)/shard_map/psum | solution.py:140
  180.1 6.7 %psum.31 = f32[8,256]{1,0:T(8,128)S(1)} all-reduce(f32[8,256]{1,0:T(8,128)S(1)} %broadcast_select_fusion.1), channel_id=1, replica_groups=mesh['slab'=8,'depth'=4] {'depth'}, use_global_device_ids=true, to_apply=%region_12.13 | all-reduce | flops 2048 | bytes 16384 | tf_op jit(solution)/shard_map/psum | solution.py:24
  187.0 11.6 %scatter_fusion.1 = f32[8,64,8]{0,2,1:T(8,128)S(1)} fusion(f32[8,64,8]{0,2,1:T(8,128)S(1)} %broadcast_in_dim.103, s32[256]{0:T(256)S(1)} %bitcast.121, f32[256,8]{1,0:T(8,128)S(1)} %copy.81), kind=kCustom, calls=%fused_computation.1 | custom fusion | bytes 26624 | tf_op jit(solution)/shard_map/scatter | solution.py:77
  198.8 0.7 reshape.473
  199.5 4.3 %all-to-all-start.1 = ((f32[8,1,512]{2,1,0:T(1,128)}), f32[8,1,512]{2,1,0:T(1,128)S(1)}, u32[]{:S(2)}, u32[]{:S(2)}) async-start(f32[8,1,512]{2,1,0:T(1,128)} %reshape.473), calls=%async_computation.1 | async-start | bytes 32768 | tf_op jit(solution)/shard_map/all_to_all | solution.py:177
  203.8 0.8 fusion.21
  204.5 5.8 %all-to-all-done.1 = f32[8,1,512]{2,1,0:T(1,128)S(1)} async-done(((f32[8,1,512]{2,1,0:T(1,128)}), f32[8,1,512]{2,1,0:T(1,128)S(1)}, u32[]{:S(2)}, u32[]{:S(2)}) %all-to-all-start.1) | async-done | bytes 16416 | tf_op jit(solution)/shard_map/all_to_all | solution.py:177
  210.3 0.5 broadcast.333
  210.8 0.7 reduce.8
  212.1 2.9 %scatter_custom_fusion.2 = f32[8,256]{0,1:T(8,128)S(1)} fusion(s32[512]{0:T(512)} %bitcast.145, f32[512,8]{1,0:T(8,128)S(1)} %copy.85, f32[]{:T(128)} %constant.114.clone.1), kind=kCustom, calls=%fused_computation.57 | custom fusion | flops 4096 | bytes 8704 | tf_op jit(solution)/shard_map/scatter-add | solution.py:90
  215.1 0.7 copy.87
  (57 shorter events, 2.3 us)
Async XLA Ops:
  0.6 124.2 %copy-start = (f32[24,24]{1,0:T(8,128)S(1)}, f32[24,24]{1,0:T(8,128)}, u32[]{:S(2)}) copy-start(f32[24,24]{1,0:T(8,128)} %param.16) | copy-start | bytes 6916
  0.6 110.5 %copy-start.3 = (f32[3,1,8,256]{3,2,1,0:T(8,128)S(1)}, f32[3,1,8,256]{3,2,1,0:T(8,128)}, u32[]{:S(2)}) copy-start(f32[3,1,8,256]{3,2,1,0:T(8,128)} %param.13) | copy-start | bytes 73732
  0.7 102.6 %copy-start.1 = (f32[3,8,1,8,256]{4,3,2,1,0:T(8,128)S(1)}, f32[3,8,1,8,256]{4,3,2,1,0:T(8,128)}, u32[]{:S(2)}) copy-start(f32[3,8,1,8,256]{4,3,2,1,0:T(8,128)} %param.12) | copy-start | bytes 589828
  2.5 100.7 %collective-permute-start.1 = (f32[28,1,8,256]{3,2,1,0:T(8,128)S(1)}, f32[28,1,8,256]{3,2,1,0:T(8,128)S(1)}, u32[]{:S(2)}, u32[]{:S(2)}) collective-permute-start(f32[28,1,8,256]{3,2,1,0:T(8,128)S(1)} %pad_maximum_fusion.1), channel_id=1, source_target_pairs={{4,0},{8,4},{12,8},{16,12},{20,16},{24,20},{28,24},{5,1},{9,5},{13... | collective-permute-start | bytes 688136 | tf_op jit(solution)/shard_map/ppermute | solution.py:17
  3.8 99.4 %collective-permute-start = (f32[28,1,8,256]{3,2,1,0:T(8,128)S(1)}, f32[28,1,8,256]{3,2,1,0:T(8,128)S(1)}, u32[]{:S(2)}, u32[]{:S(2)}) collective-permute-start(f32[28,1,8,256]{3,2,1,0:T(8,128)S(1)} %pad_maximum_fusion.1), channel_id=1, source_target_pairs={{0,4},{4,8},{8,12},{12,16},{16,20},{20,24},{24,28},{1,5},{5,9},{9,... | collective-permute-start | bytes 688136 | tf_op jit(solution)/shard_map/ppermute | solution.py:16
  51.6 51.4 %all-to-all-start = ((f32[1,64,8]{1,0,2:T(1,128)}), f32[1,64,8]{1,0,2:T(1,128)S(1)}, u32[]{:S(2)}, u32[]{:S(2)}) async-start(f32[1,64,8]{1,0,2:T(1,128)} %bitcast.34), calls=%async_computation | async-start | bytes 8192 | tf_op jit(solution)/shard_map/all_to_all | solution.py:178
  101.0 0.6 copy-start.6
  104.1 3.1 %collective-permute-start.2 = (f32[28,3,1,256]{3,2,1,0:T(1,128)S(1)}, f32[28,3,1,256]{3,2,1,0:T(1,128)S(1)}, u32[]{:S(2)}, u32[]{:S(2)}) collective-permute-start(f32[28,3,1,256]{3,2,1,0:T(1,128)S(1)} %get-tuple-element.43), channel_id=1, source_target_pairs={{0,1},{1,2},{2,3},{4,5},{5,6},{6,7},{8,9},{9,10},{10,11},{12,13},{... | collective-permute-start | bytes 258056 | tf_op jit(solution)/shard_map/ppermute | solution.py:16
  105.4 5.7 %collective-permute-start.3 = (f32[28,3,1,256]{3,2,1,0:T(1,128)S(1)}, f32[28,3,1,256]{3,2,1,0:T(1,128)S(1)}, u32[]{:S(2)}, u32[]{:S(2)}) collective-permute-start(f32[28,3,1,256]{3,2,1,0:T(1,128)S(1)} %get-tuple-element.44), channel_id=1, source_target_pairs={{1,0},{2,1},{3,2},{5,4},{6,5},{7,6},{9,8},{10,9},{11,10},{13,12},{... | collective-permute-start | bytes 258056 | tf_op jit(solution)/shard_map/ppermute | solution.py:17
  129.8 5.2 %copy-start.5 = (f32[2,9,256]{2,1,0:T(8,128)S(1)}, f32[2,9,256]{2,1,0:T(8,128)}, u32[]{:S(2)}) copy-start(f32[2,9,256]{2,1,0:T(8,128)} %slice.139) | copy-start | bytes 55300
  135.0 3.7 %copy-start.2 = (f32[3,8,1,8,256]{4,3,2,1,0:T(8,128)S(1)}, f32[3,8,1,8,256]{4,3,2,1,0:T(8,128)}, u32[]{:S(2)}) copy-start(f32[3,8,1,8,256]{4,3,2,1,0:T(8,128)} %param.12) | copy-start | bytes 589828
  135.0 3.7 %copy-start.4 = (f32[3,1,8,256]{3,2,1,0:T(8,128)S(1)}, f32[3,1,8,256]{3,2,1,0:T(8,128)}, u32[]{:S(2)}) copy-start(f32[3,1,8,256]{3,2,1,0:T(8,128)} %param.13) | copy-start | bytes 73732
  135.0 3.7 %copy-start.7 = (f32[1,3,8]{2,1,0:T(4,128)S(1)}, f32[1,3,8]{2,1,0:T(4,128)}, u32[]{:S(2)}) copy-start(f32[1,3,8]{2,1,0:T(4,128)} %copy-done.6) | copy-start | bytes 292
  138.7 41.3 %copy-start.8 = (f32[3,1,256]{2,0,1:T(4,128)S(1)}, f32[3,1,256]{2,0,1:T(4,128)}, u32[]{:S(2)}) copy-start(f32[3,1,256]{2,0,1:T(4,128)} %copy.99) | copy-start | bytes 9220
  199.5 10.8 %all-to-all-start.1 = ((f32[8,1,512]{2,1,0:T(1,128)}), f32[8,1,512]{2,1,0:T(1,128)S(1)}, u32[]{:S(2)}, u32[]{:S(2)}) async-start(f32[8,1,512]{2,1,0:T(1,128)} %reshape.473), calls=%async_computation.1 | async-start | bytes 32768 | tf_op jit(solution)/shard_map/all_to_all | solution.py:177
where the time goes:
time: 218 us; the launch traced here: 216 us
  blocking collectives  88.4 us (41%)
  local copies, waits for them, and re-layouts  74.5 us (34%)
  starting transfers between devices  19.9 us (9%)
  other arithmetic  16.4 us (8%)
  waiting for transfers between devices  9.68 us (4%)
  matrix products  5.84 us (3%)
    psum x1, blocking collectives, body(): lax.psum(jnp.sum(right_side * direction, axis=(0, 2, 3, 4)), ('slab', 'de...  40.8 us
    psum x1, blocking collectives, body(): coarse_sum = lax.psum(placed, ('slab', 'depth'))  40.8 us
    scatter x1, local copies, waits for them, and re-layouts, pack_slots(): send_ids = jnp.zeros((1, capacity, n_slab), jnp.float32).at[0, slot_rank,...  38.7 us
    scatter x2, local copies, waits for them, and re-layouts, pack_slots(): send_vals = jnp.zeros((values.shape[0], capacity, n_slab), jnp.float32).a...  11.8 us
    unnamed x29, local copies, waits for them, and re-layouts  10.8 us
    ppermute x2, starting transfers between devices, extended(): before = lax.ppermute(last, axis, up)  6.81 us
    psum x1, blocking collectives, broadcast(): return lax.psum(kept, axis)  6.75 us
    all_to_all x1, starting transfers between devices, body(): lax.all_to_all(send_ids, 'slab', split_axis=2, concat_axis=2, tiled=True)  6.2 us
  transfers between devices with their start and end apart: 6, of which 2 were waited for; matrix products, arithmetic and copies ran while one was open for 22% of the time, Pallas kernels for 0%

commit v1 on v0

--- a/solution.py
+++ b/solution.py
@@ -126,7 +126,7 @@
         jnp.arange(n_slab, dtype=jnp.int32)[:, None, None] == slab_rank, block_sums[None], 0.0
     )
     placed = placed.reshape(components * n_slab, sources)
-    coarse_sum = lax.psum(placed, ("slab", "depth"))
+    coarse_sum = jnp.sum(lax.all_gather(placed, ("slab", "depth")), axis=0)
     coarse_vec = coarse_sum / agg_nodes
     correction = jnp.dot(
         coarse_inverse,

time: 218 us -> 213 us (0.977)
  waiting for transfers between devices: 9.68 us -> 7.16 us
    all_gather x0 -> x1, blocking collectives: none -> 42.3 us  [body(): coarse_sum = jnp.sum(lax.all_gather(placed, ('slab', 'depth')), axis=0)]
    psum x1 -> x0, blocking collectives: 40.8 us -> none  [body(): coarse_sum = lax.psum(placed, ('slab', 'depth'))]
    psum x1, blocking collectives: 40.8 us -> 37.5 us  [body(): lax.psum(jnp.sum(right_side * direction, axis=(0, 2, 3, 4)), ('slab', 'de...]
    ppermute x2, waiting for transfers between devices: 3.86 us -> 1.34 us  [extended(): after = lax.ppermute(initial, axis, down)]
    unnamed x29 -> x31, local copies, waits for them, and re-layouts: 10.8 us -> 10.1 us
where the time goes in v1:
time: 213 us; the launch traced here: 212 us
  blocking collectives  87 us (41%)
  local copies, waits for them, and re-layouts  73.9 us (35%)
  starting transfers between devices  21 us (10%)
  other arithmetic  15.7 us (7%)
  waiting for transfers between devices  7.16 us (3%)
  matrix products  5.78 us (3%)
    all_gather x1, blocking collectives, body(): coarse_sum = jnp.sum(lax.all_gather(placed, ('slab', 'depth')), axis=0)  42.3 us
    scatter x1, local copies, waits for them, and re-layouts, pack_slots(): send_ids = jnp.zeros((1, capacity, n_slab), jnp.float32).at[0, slot_rank,...  38.7 us
    psum x1, blocking collectives, body(): lax.psum(jnp.sum(right_side * direction, axis=(0, 2, 3, 4)), ('slab', 'de...  37.5 us
    scatter x2, local copies, waits for them, and re-layouts, pack_slots(): send_vals = jnp.zeros((values.shape[0], capacity, n_slab), jnp.float32).a...  11.8 us
    unnamed x31, local copies, waits for them, and re-layouts  10.1 us
    ppermute x2, starting transfers between devices, extended(): before = lax.ppermute(last, axis, up)  7.77 us
    psum x1, blocking collectives, broadcast(): return lax.psum(kept, axis)  7.21 us
    all_to_all x1, starting transfers between devices, body(): lax.all_to_all(send_ids, 'slab', split_axis=2, concat_axis=2, tiled=True)  6.2 us
  transfers between devices with their start and end apart: 6, of which 2 were waited for; matrix products, arithmetic and copies ran while one was open for 22% of the time, Pallas kernels for 0%

profile of v1, /device:TPU:0, one launch (start us, length us, event | category | flops | bytes accessed | tf_op | source)
XLA Modules:
  0.0 211.6 jit_solution(544142934179366257)
XLA Ops:
  0.7 0.8 select_reduce_fusion
  1.5 1.0 pad_maximum_fusion.1
  2.5 1.3 collective-permute-start.1
  3.8 5.5 %collective-permute-start = (f32[28,1,8,256]{3,2,1,0:T(8,128)S(1)}, f32[28,1,8,256]{3,2,1,0:T(8,128)S(1)}, u32[]{:S(2)}, u32[]{:S(2)}) collective-permute-start(f32[28,1,8,256]{3,2,1,0:T(8,128)S(1)} %pad_maximum_fusion.1), channel_id=1, source_target_pairs={{0,4},{4,8},{8,12},{12,16},{16,20},{20,24},{24,28},{1,5},{5,9},{9,... | collective-permute-start | bytes 688136 | tf_op jit(solution)/shard_map/ppermute | solution.py:16
  9.3 0.7 and_select_fusion.2
  10.0 0.7 fusion.34
  10.7 0.6 reduce-window.6
  11.3 0.2 slice_reduce_fusion
  11.6 0.7 or_select_fusion
  12.3 0.6 broadcast.335
  12.9 38.7 %scatter_fusion = f32[64,8]{0,1:T(8,128)} fusion(f32[64,8]{0,1:T(8,128)} %broadcast.335, s32[256]{0:T(256)S(1)} %bitcast.120, f32[256]{0:T(256)S(1)} %get-tuple-element.51), kind=kCustom, calls=%fused_computation | custom fusion | bytes 5120 | tf_op jit(solution)/shard_map/scatter | solution.py:82
  51.6 6.2 %all-to-all-start = ((f32[1,64,8]{1,0,2:T(1,128)}), f32[1,64,8]{1,0,2:T(1,128)S(1)}, u32[]{:S(2)}, u32[]{:S(2)}) async-start(f32[1,64,8]{1,0,2:T(1,128)} %bitcast.34), calls=%async_computation | async-start | bytes 8192 | tf_op jit(solution)/shard_map/all_to_all | solution.py:178
  57.8 1.1 reduce_sum.65
  59.3 42.3 %all_gather.3 = f32[32,24,8]{1,2,0:T(8,128)S(1)} all-gather(f32[1,24,8]{1,2,0:T(8,128)S(1)} %copy.93), channel_id=1, replica_groups=mesh['slab'=8,'depth'=4] {'slab','depth'}, dimensions={0}, use_global_device_ids=true | all-gather | bytes 25344 | tf_op jit(solution)/shard_map/all_gather | solution.py:129
  101.6 0.8 convolution_bitcast_fusion.1
  102.7 0.4 copy-done.6
  103.2 0.6 copy.121
  104.2 2.3 %collective-permute-start.2 = (f32[28,3,1,256]{3,2,1,0:T(1,128)S(1)}, f32[28,3,1,256]{3,2,1,0:T(1,128)S(1)}, u32[]{:S(2)}, u32[]{:S(2)}) collective-permute-start(f32[28,3,1,256]{3,2,1,0:T(1,128)S(1)} %get-tuple-element.45), channel_id=1, source_target_pairs={{0,1},{1,2},{2,3},{4,5},{5,6},{6,7},{8,9},{9,10},{10,11},{12,13},{... | collective-permute-start | bytes 258056 | tf_op jit(solution)/shard_map/ppermute | solution.py:16
  106.5 1.3 collective-permute-start.3
  107.8 0.5 compare_select_fusion
  108.3 1.3 collective-permute-done.3
  109.6 0.6 slice.139
  110.3 0.3 pad_maximum_fusion
  110.7 0.3 multiply_add_fusion
  110.9 1.1 fusion.1
  112.1 1.0 fusion.11
  113.1 1.2 fusion.3
  114.2 1.0 fusion.10
  115.2 1.1 fusion.5
  116.4 0.9 fusion.9
  117.3 1.2 fusion.7
  118.5 1.0 fusion.8
  119.5 3.8 %reshape.469 = f32[24,36864]{1,0:T(8,128)S(1)} reshape(f32[8,3,8,2,9,256]{5,4,3,2,1,0:T(8,128)} %fusion.8) | data formatting | bytes 7077888 | tf_op jit(solution)/shard_map/reshape | solution.py:44
  123.3 4.9 %convolution_bitcast_fusion = f32[24,36864]{1,0:T(8,128)} fusion(f32[24,36864]{1,0:T(8,128)S(1)} %reshape.469, f32[24,24]{1,0:T(8,128)S(1)} %copy-done), kind=kOutput, calls=%fused_computation.3 | convolution fusion | flops 254803968 | bytes 7080192 | tf_op jit(solution)/shard_map/dot_general | solution.py:45
  128.3 5.2 %reshape.470 = f32[8,3,8,2,9,256]{5,4,3,2,1,0:T(8,128)} reshape(f32[24,36864]{1,0:T(8,128)} %convolution_bitcast_fusion) | data formatting | bytes 7077888 | tf_op jit(solution)/shard_map/reshape | solution.py:48
  133.5 3.6 %broadcast_multiply_fusion = f32[8,3,8,2,9,256]{5,4,3,2,1,0:T(8,128)S(1)} fusion(f32[8,3,8,2,9,256]{5,4,3,2,1,0:T(8,128)} %reshape.470, f32[2,9,256]{2,1,0:T(8,128)S(1)} %copy-done.5), kind=kLoop, calls=%fused_computation.8 | loop fusion | flops 884736 | bytes 7096320 | tf_op jit(solution)/shard_map/mul | solution.py:48
  137.2 0.4 fusion.19
  137.6 37.5 %all-reduce.3 = (f32[8]{0:T(128)S(1)}, f32[8]{0:T(128)S(1)}) all-reduce(f32[8]{0:T(128)S(1)} %get-tuple-element.41, f32[8]{0:T(128)S(1)} %get-tuple-element.40), channel_id=1, replica_groups=mesh['slab'=8,'depth'=4] {'slab','depth'}, use_global_device_ids=true, to_apply=%region_3.4 | all-reduce | flops 16 | bytes 128 | tf_op jit(solution)/shard_map/psum | solution.py:140
  175.2 7.2 %psum.23 = f32[8,256]{1,0:T(8,128)S(1)} all-reduce(f32[8,256]{1,0:T(8,128)S(1)} %broadcast_select_fusion.1), channel_id=1, replica_groups=mesh['slab'=8,'depth'=4] {'depth'}, use_global_device_ids=true, to_apply=%region_12.13 | all-reduce | flops 2048 | bytes 16384 | tf_op jit(solution)/shard_map/psum | solution.py:24
  182.6 11.6 %scatter_fusion.1 = f32[8,64,8]{0,2,1:T(8,128)S(1)} fusion(f32[8,64,8]{0,2,1:T(8,128)S(1)} %broadcast_in_dim.103, s32[256]{0:T(256)S(1)} %bitcast.121, f32[256,8]{1,0:T(8,128)S(1)} %copy.102), kind=kCustom, calls=%fused_computation.1 | custom fusion | bytes 26624 | tf_op jit(solution)/shard_map/scatter | solution.py:77
  194.4 0.7 reshape.504
  195.1 4.5 %all-to-all-start.1 = ((f32[8,1,512]{2,1,0:T(1,128)}), f32[8,1,512]{2,1,0:T(1,128)S(1)}, u32[]{:S(2)}, u32[]{:S(2)}) async-start(f32[8,1,512]{2,1,0:T(1,128)} %reshape.504), calls=%async_computation.1 | async-start | bytes 32768 | tf_op jit(solution)/shard_map/all_to_all | solution.py:177
  199.6 0.8 fusion.21
  200.3 5.8 %all-to-all-done.1 = f32[8,1,512]{2,1,0:T(1,128)S(1)} async-done(((f32[8,1,512]{2,1,0:T(1,128)}), f32[8,1,512]{2,1,0:T(1,128)S(1)}, u32[]{:S(2)}, u32[]{:S(2)}) %all-to-all-start.1) | async-done | bytes 16416 | tf_op jit(solution)/shard_map/all_to_all | solution.py:177
  206.1 0.5 broadcast.352
  206.7 0.7 reduce.8
  207.9 2.9 %scatter_custom_fusion.2 = f32[8,256]{0,1:T(8,128)S(1)} fusion(s32[512]{0:T(512)} %bitcast.145, f32[512,8]{1,0:T(8,128)S(1)} %copy.106, f32[]{:T(128)} %constant.114.clone.1), kind=kCustom, calls=%fused_computation.57 | custom fusion | flops 4096 | bytes 8704 | tf_op jit(solution)/shard_map/scatter-add | solution.py:90
  210.9 0.7 copy.108
  (61 shorter events, 2.3 us)
Async XLA Ops:
  0.6 122.7 %copy-start = (f32[24,24]{1,0:T(8,128)S(1)}, f32[24,24]{1,0:T(8,128)}, u32[]{:S(2)}) copy-start(f32[24,24]{1,0:T(8,128)} %param.16) | copy-start | bytes 6916
  0.6 103.4 %copy-start.3 = (f32[3,1,8,256]{3,2,1,0:T(8,128)S(1)}, f32[3,1,8,256]{3,2,1,0:T(8,128)}, u32[]{:S(2)}) copy-start(f32[3,1,8,256]{3,2,1,0:T(8,128)} %param.13) | copy-start | bytes 73732
  0.7 103.4 %copy-start.1 = (f32[3,8,1,8,256]{4,3,2,1,0:T(8,128)S(1)}, f32[3,8,1,8,256]{4,3,2,1,0:T(8,128)}, u32[]{:S(2)}) copy-start(f32[3,8,1,8,256]{4,3,2,1,0:T(8,128)} %param.12) | copy-start | bytes 589828
  0.7 102.6 %copy-start.9 = (f32[3,1,256]{2,1,0:T(1,128)S(1)}, f32[3,1,256]{2,1,0:T(1,128)}, u32[]{:S(2)}) copy-start(f32[3,1,256]{2,1,0:T(1,128)} %param.19) | copy-start | bytes 9220
  2.5 101.5 %collective-permute-start.1 = (f32[28,1,8,256]{3,2,1,0:T(8,128)S(1)}, f32[28,1,8,256]{3,2,1,0:T(8,128)S(1)}, u32[]{:S(2)}, u32[]{:S(2)}) collective-permute-start(f32[28,1,8,256]{3,2,1,0:T(8,128)S(1)} %pad_maximum_fusion.1), channel_id=1, source_target_pairs={{4,0},{8,4},{12,8},{16,12},{20,16},{24,20},{28,24},{5,1},{9,5},{13... | collective-permute-start | bytes 688136 | tf_op jit(solution)/shard_map/ppermute | solution.py:17
  3.8 100.3 %collective-permute-start = (f32[28,1,8,256]{3,2,1,0:T(8,128)S(1)}, f32[28,1,8,256]{3,2,1,0:T(8,128)S(1)}, u32[]{:S(2)}, u32[]{:S(2)}) collective-permute-start(f32[28,1,8,256]{3,2,1,0:T(8,128)S(1)} %pad_maximum_fusion.1), channel_id=1, source_target_pairs={{0,4},{4,8},{8,12},{12,16},{16,20},{20,24},{24,28},{1,5},{5,9},{9,... | collective-permute-start | bytes 688136 | tf_op jit(solution)/shard_map/ppermute | solution.py:16
  51.6 52.2 %all-to-all-start = ((f32[1,64,8]{1,0,2:T(1,128)}), f32[1,64,8]{1,0,2:T(1,128)S(1)}, u32[]{:S(2)}, u32[]{:S(2)}) async-start(f32[1,64,8]{1,0,2:T(1,128)} %bitcast.34), calls=%async_computation | async-start | bytes 8192 | tf_op jit(solution)/shard_map/all_to_all | solution.py:178
  102.5 0.6 copy-start.6
  104.2 4.1 %collective-permute-start.2 = (f32[28,3,1,256]{3,2,1,0:T(1,128)S(1)}, f32[28,3,1,256]{3,2,1,0:T(1,128)S(1)}, u32[]{:S(2)}, u32[]{:S(2)}) collective-permute-start(f32[28,3,1,256]{3,2,1,0:T(1,128)S(1)} %get-tuple-element.45), channel_id=1, source_target_pairs={{0,1},{1,2},{2,3},{4,5},{5,6},{6,7},{8,9},{9,10},{10,11},{12,13},{... | collective-permute-start | bytes 258056 | tf_op jit(solution)/shard_map/ppermute | solution.py:16
  106.5 3.2 %collective-permute-start.3 = (f32[28,3,1,256]{3,2,1,0:T(1,128)S(1)}, f32[28,3,1,256]{3,2,1,0:T(1,128)S(1)}, u32[]{:S(2)}, u32[]{:S(2)}) collective-permute-start(f32[28,3,1,256]{3,2,1,0:T(1,128)S(1)} %get-tuple-element.46), channel_id=1, source_target_pairs={{1,0},{2,1},{3,2},{5,4},{6,5},{7,6},{9,8},{10,9},{11,10},{13,12},{... | collective-permute-start | bytes 258056 | tf_op jit(solution)/shard_map/ppermute | solution.py:17
  128.3 5.2 %copy-start.5 = (f32[2,9,256]{2,1,0:T(8,128)S(1)}, f32[2,9,256]{2,1,0:T(8,128)}, u32[]{:S(2)}) copy-start(f32[2,9,256]{2,1,0:T(8,128)} %slice.139) | copy-start | bytes 55300
  133.5 3.7 %copy-start.2 = (f32[3,8,1,8,256]{4,3,2,1,0:T(8,128)S(1)}, f32[3,8,1,8,256]{4,3,2,1,0:T(8,128)}, u32[]{:S(2)}) copy-start(f32[3,8,1,8,256]{4,3,2,1,0:T(8,128)} %param.12) | copy-start | bytes 589828
  133.5 3.7 %copy-start.4 = (f32[3,1,8,256]{3,2,1,0:T(8,128)S(1)}, f32[3,1,8,256]{3,2,1,0:T(8,128)}, u32[]{:S(2)}) copy-start(f32[3,1,8,256]{3,2,1,0:T(8,128)} %param.13) | copy-start | bytes 73732
  133.5 3.7 %copy-start.7 = (f32[1,3,8]{2,1,0:T(4,128)S(1)}, f32[1,3,8]{2,1,0:T(4,128)}, u32[]{:S(2)}) copy-start(f32[1,3,8]{2,1,0:T(4,128)} %copy-done.6) | copy-start | bytes 292
  137.2 37.9 %copy-start.8 = (f32[3,1,256]{2,0,1:T(4,128)S(1)}, f32[3,1,256]{2,0,1:T(4,128)}, u32[]{:S(2)}) copy-start(f32[3,1,256]{2,0,1:T(4,128)} %copy.121) | copy-start | bytes 9220
  195.1 11.1 %all-to-all-start.1 = ((f32[8,1,512]{2,1,0:T(1,128)}), f32[8,1,512]{2,1,0:T(1,128)S(1)}, u32[]{:S(2)}, u32[]{:S(2)}) async-start(f32[8,1,512]{2,1,0:T(1,128)} %reshape.504), calls=%async_computation.1 | async-start | bytes 32768 | tf_op jit(solution)/shard_map/all_to_all | solution.py:177
